TPU v7x, 256 devices: a whole 4x4x8 slice. The times are simulated.
256 devices in a mesh: tm: 16 (over y_lo, x, core), blk: 8 (over z), samp: 2 (over y_hi).
Axes of the slice: x: 4, y: 4 (y_hi: 2, y_lo: 2; y = y_hi * 2 + y_lo), z: 8, core: 2. Of those that a mesh axis runs over, the one named last changes fastest.
Arguments:
- prior_path: float32 [32, 16, 1024], P('tm', 'samp', 'blk'), may hold values from -6 to 6
- observed: float32 [32, 256], P('tm', 'blk'), may hold values from -6 to 6
- obs_mask: int32 [32, 32], P('tm', 'blk'), may hold values 0 or 1
- noise_draw: float32 [32, 16, 256], P('tm', 'samp', 'blk'), may hold values from -6 to 6
- wend_blocks: float32 [128, 8, 8], P('blk'), may hold values from -1 to 1
- block_cols: int32 [128], P('blk'), may hold values from 0 to 31, as said below
- start_mean: float32 [16, 1024], P('samp', 'blk'), may hold values from -6 to 6
- trans_mats: bfloat16 [32, 1024, 1024], P('tm', 'blk', 'samp')
- gain_mats: bfloat16 [32, 1024, 256], P('tm', 'blk', 'samp'), may hold values from -0.375 to 0.375
- smooth_mats: bfloat16 [32, 1024, 1024], P('tm', 'blk', 'samp')
- site_trans: float32 [4, 4], replicated, may hold values from -2.5 to 2.5
Outputs:
- posterior_path: float32 [32, 16, 1024], P('tm', 'samp', 'blk')
Inputs may be any that keep to these rules, and one draw needn't show every extreme that they name: `block_cols`: entry 4 i names block i itself, entries 4 i + 1 to 4 i + 3 name three different blocks among i - 2, i - 1, i + 1, i + 2 taken modulo 32.
All inputs are finite; a program needn't handle non-finite values. No bound on the sum of `obs_mask` on one device may be relied on, other than what follows from the above.
Results may differ from a plain program's by a relative error of at most 0.0003.
Values may be sent and summed in bfloat16 or wider, within the bound.
No kernel may reach another device: no remote copies, remote signals or barrier semaphores. Data moves between devices by JAX's collectives and lax.ppermute only.
A program may use at most 64 MiB of HBM per device.

v0:
```python
import jax
import jax.numpy as jnp
from jax import lax
from jax.sharding import PartitionSpec as P

highest = lax.Precision.HIGHEST


def with_halo(value, sides, width):
    for axis, dim in sides:
        count, length = (lax.axis_size(axis), value.shape[dim])
        up = [(i, (i + 1) % count) for i in range(count)]
        down = [(j, i) for i, j in up]
        last = lax.slice_in_dim(value, length - width, length, axis=dim)
        initial = lax.slice_in_dim(value, 0, width, axis=dim)
        before = lax.ppermute(last, axis, up)
        after = lax.ppermute(initial, axis, down)
        value = jnp.concatenate([before, value, after], axis=dim)
    return value


def shifted(value, axis, steps):
    count = lax.axis_size(axis)
    initial, last = (max(0, -steps), min(count, count - steps))
    return lax.ppermute(value, axis, [(source, source + steps) for source in range(initial, last)])


def apply_rows(matrix, states):
    return jnp.einsum("ij,sj->si", matrix, states, precision=highest)


def on_device(
    prior_path,
    observed,
    obs_mask,
    noise_draw,
    wend_blocks,
    block_cols,
    start_mean,
    trans_mats,
    gain_mats,
    smooth_mats,
    site_trans,
):
    trans_mats, gain_mats, smooth_mats = (
        lax.all_gather(trans_mats, "samp", axis=2, tiled=True),
        lax.all_gather(gain_mats, "samp", axis=2, tiled=True),
        lax.all_gather(smooth_mats, "samp", axis=2, tiled=True),
    )
    step_count, sample_count, local_sites = noise_draw.shape
    block_sites = wend_blocks.shape[1]
    local_blocks = local_sites // block_sites
    cycle_size = lax.axis_size("blk")
    block_count = local_blocks * cycle_size
    row_count = trans_mats.shape[1]
    state_count = row_count * cycle_size
    widened = with_halo(noise_draw, (("blk", 2),), 2 * block_sites)
    rim_blocks = widened.reshape(step_count, sample_count, local_blocks + 4, block_sites)
    pair_rows = jnp.arange(local_blocks * 4, dtype=jnp.int32) // 4
    first_block = lax.axis_index("blk") * local_blocks
    offset = (block_cols - first_block - pair_rows + 2) % block_count
    position = pair_rows + offset
    chooser = (position[:, None] == jnp.arange(local_blocks + 4, dtype=jnp.int32)[None, :]).astype(
        jnp.float32
    )
    picked = jnp.einsum("pl,tslj->tspj", chooser, rim_blocks, precision=highest)
    mixed = jnp.einsum("tspj,pij->tspi", picked, wend_blocks, precision=highest)
    obs_noise = jnp.sum(
        mixed.reshape(step_count, sample_count, local_blocks, 4, block_sites), axis=3
    ).reshape(step_count, sample_count, local_sites)
    first_comp = prior_path.reshape(step_count, sample_count, local_sites, 4)[:, :, :, 0]
    seen_mask = jnp.repeat(obs_mask.astype(jnp.float32), block_sites, axis=1)
    residual = seen_mask[:, None, :] * (observed[:, None, :] - first_comp - obs_noise)
    all_resid = lax.all_gather(residual, "blk", axis=2, tiled=True)
    inputs = jnp.einsum("tij,tsj->tsi", gain_mats, all_resid, precision=highest)
    left_trans = trans_mats[1]
    left_smooth = smooth_mats[0]
    forward_pair = jnp.dot(
        left_trans,
        lax.all_gather(trans_mats[0], "blk", axis=0, tiled=True),
        preferred_element_type=jnp.float32,
    )
    backward_pair = jnp.dot(
        left_smooth,
        lax.all_gather(smooth_mats[1], "blk", axis=0, tiled=True),
        preferred_element_type=jnp.float32,
    )
    first_input, initial = (
        lax.all_gather(inputs[0], "blk", axis=1, tiled=True),
        lax.all_gather(start_mean, "blk", axis=1, tiled=True),
    )
    carry_input = apply_rows(trans_mats[1], first_input) + inputs[1]
    is_first = lax.axis_index("tm") == 0
    time_size = lax.axis_size("tm")
    level_count = (time_size - 1).bit_length()
    matrix, vector = shifted((forward_pair, carry_input), "tm", 1)
    vector = jnp.where(is_first, start_mean, vector)
    for level in range(level_count):
        received_m, received_v = shifted((matrix, vector), "tm", 1 << level)
        complete_m, complete_v = (
            lax.all_gather(received_m, "blk", axis=0, tiled=True),
            lax.all_gather(received_v, "blk", axis=1, tiled=True),
        )
        matrix, vector = (
            jnp.dot(matrix, complete_m, precision=highest),
            apply_rows(matrix, complete_v) + vector,
        )
    entry_state = lax.all_gather(vector, "blk", axis=1, tiled=True)
    filtered = jnp.stack(
        [
            apply_rows(trans_mats[0], entry_state) + inputs[0],
            apply_rows(forward_pair, entry_state) + carry_input,
        ]
    )
    site_kron = jnp.kron(jnp.eye(row_count // 4, dtype=jnp.float32), site_trans)
    predicted = jnp.einsum("ij,tsj->tsi", site_kron, filtered, precision=highest)
    all_pred = lax.all_gather(predicted, "blk", axis=2, tiled=True)
    offsets = filtered - jnp.einsum("tij,tsj->tsi", smooth_mats, all_pred, precision=highest)
    is_last = lax.axis_index("tm") == time_size - 1
    late_offset = jnp.where(is_last, filtered[1], offsets[1])
    all_late = lax.all_gather(late_offset, "blk", axis=1, tiled=True)
    back_offset = apply_rows(smooth_mats[0], all_late) + offsets[0]

    def relay_back(relay_turn, later_now):
        emitted = apply_rows(backward_pair, later_now) + back_offset
        complete = lax.all_gather(emitted, "blk", axis=1, tiled=True)
        received = shifted(complete, "tm", -1)
        return jnp.where(lax.axis_index("tm") == time_size - 2 - relay_turn, received, later_now)

    later_state = lax.fori_loop(
        0, time_size - 1, relay_back, jnp.zeros((sample_count, state_count), jnp.float32)
    )
    smoothed = jnp.stack(
        [
            apply_rows(backward_pair, later_state) + back_offset,
            apply_rows(smooth_mats[1], later_state) + late_offset,
        ]
    )
    return prior_path + smoothed


def solution(mesh):
    placed = (
        P("tm", "samp", "blk"),
        P("tm", "blk"),
        P("tm", "blk"),
        P("tm", "samp", "blk"),
        P("blk", None, None),
        P("blk"),
        P("samp", "blk"),
        P("tm", "blk", "samp"),
        P("tm", "blk", "samp"),
        P("tm", "blk", "samp"),
        P(),
    )
    return jax.shard_map(
        on_device, mesh=mesh, in_specs=placed, out_specs=P("tm", "samp", "blk"), check_vma=False
    )
```

profile of v0, /device:TPU:7, one launch (start us, length us, event | category | flops | bytes accessed | tf_op | source)
XLA Modules:
  0.0 952.8 jit_solution(16144380244082695753)
XLA Ops:
  16.9 41.3 %all-gather.17.cloned.1.call-done = bf16[1,1024,1024]{2,1,0:T(8,128)(2,1)} async-done(((bf16[1,128,1024]{2,1,0:T(8,128)(2,1)}), bf16[1,1024,1024]{2,1,0:T(8,128)(2,1)}) %all-gather.17.cloned.1.call-update) | async-done | bytes 2097168 | tf_op jit(solution)/shard_map/all_gather | solution.py:80
  87.2 53.6 %all-gather.9.cloned.1.call-done = f32[1024,1024]{1,0:T(8,128)} async-done(((f32[128,1024]{1,0:T(8,128)}), f32[1024,1024]{1,0:T(8,128)}) %all-gather.9.cloned.1.call-update) | async-done | bytes 4194320 | tf_op jit(solution)/shard_map/all_gather | solution.py:101
  148.7 11.6 %collective-permute-done.9 = f32[128,1024]{1,0:T(8,128)S(1)} collective-permute-done((f32[128,1024]{1,0:T(8,128)S(1)}, f32[128,1024]{1,0:T(8,128)S(1)}, u32[]{:S(2)}, u32[]{:S(2)}) %collective-permute-start.9) | collective-permute-done | bytes 524320 | tf_op jit(solution)/shard_map/ppermute | solution.py:25
  170.5 45.1 %all-gather.11.cloned.1.call-done = f32[1024,1024]{1,0:T(8,128)} async-done(((f32[128,1024]{1,0:T(8,128)}), f32[1024,1024]{1,0:T(8,128)}) %all-gather.11.cloned.1.call-update) | async-done | bytes 4194320 | tf_op jit(solution)/shard_map/all_gather | solution.py:101
  224.2 12.2 %collective-permute-done.11 = f32[128,1024]{1,0:T(8,128)S(1)} collective-permute-done((f32[128,1024]{1,0:T(8,128)S(1)}, f32[128,1024]{1,0:T(8,128)S(1)}, u32[]{:S(2)}, u32[]{:S(2)}) %collective-permute-start.11) | collective-permute-done | bytes 524320 | tf_op jit(solution)/shard_map/ppermute | solution.py:25
  246.9 19.8 %all_gather.60 = f32[2,8,256]{1,0,2:T(2,128)S(1)} all-gather(f32[2,8,32]{1,0,2:T(2,128)S(1)} %copy.27), channel_id=1, replica_groups=mesh['tm'=16,'blk'=8,'samp'=2] {'blk'}, dimensions={2}, use_global_device_ids=true | all-gather | bytes 18432 | tf_op jit(solution)/shard_map/all_gather | solution.py:74
  267.0 20.3 %all-gather.1 = f32[1,8,1024]{2,1,0:T(8,128)S(1)} all-gather(f32[1,8,128]{2,1,0:T(8,128)S(1)} %slice.52), channel_id=3, replica_groups=mesh['tm'=16,'blk'=8,'samp'=2] {'blk'}, dimensions={2}, use_global_device_ids=true | all-gather | bytes 36864 | tf_op jit(solution)/shard_map/all_gather | solution.py:89
  287.5 16.8 %collective-permute-start.3 = (f32[8,128]{1,0:T(8,128)S(1)}, f32[8,128]{1,0:T(8,128)S(1)}, u32[]{:S(2)}, u32[]{:S(2)}) collective-permute-start(f32[8,128]{1,0:T(8,128)S(1)} %convolution_add_fusion.4), channel_id=1, source_target_pairs={{0,16},{16,32},{32,48},{48,64},{64,80},{80,96},{96,112},{112,128},... | collective-permute-start | bytes 12296 | tf_op jit(solution)/shard_map/ppermute | solution.py:25
  312.1 18.1 %all_gather.64 = f32[8,1024]{1,0:T(8,128)S(1)} all-gather(f32[8,128]{1,0:T(8,128)S(1)} %collective-permute-done.4), channel_id=1, replica_groups=mesh['tm'=16,'blk'=8,'samp'=2] {'blk'}, dimensions={1}, use_global_device_ids=true | all-gather | bytes 36864 | tf_op jit(solution)/shard_map/all_gather | solution.py:102
  335.1 18.1 %all_gather.66 = f32[8,1024]{1,0:T(8,128)S(1)} all-gather(f32[8,128]{1,0:T(8,128)S(1)} %collective-permute-done.6), channel_id=1, replica_groups=mesh['tm'=16,'blk'=8,'samp'=2] {'blk'}, dimensions={1}, use_global_device_ids=true | all-gather | bytes 36864 | tf_op jit(solution)/shard_map/all_gather | solution.py:102
  359.5 18.3 %all_gather.68 = f32[8,1024]{1,0:T(8,128)S(1)} all-gather(f32[8,128]{1,0:T(8,128)S(1)} %collective-permute-done.8), channel_id=1, replica_groups=mesh['tm'=16,'blk'=8,'samp'=2] {'blk'}, dimensions={1}, use_global_device_ids=true | all-gather | bytes 36864 | tf_op jit(solution)/shard_map/all_gather | solution.py:102
  381.8 18.1 %all_gather.70 = f32[8,1024]{1,0:T(8,128)S(1)} all-gather(f32[8,128]{1,0:T(8,128)S(1)} %collective-permute-done.10), channel_id=1, replica_groups=mesh['tm'=16,'blk'=8,'samp'=2] {'blk'}, dimensions={1}, use_global_device_ids=true | all-gather | bytes 36864 | tf_op jit(solution)/shard_map/all_gather | solution.py:102
  405.0 18.2 %all_gather.72 = f32[8,1024]{1,0:T(8,128)S(1)} all-gather(f32[8,128]{1,0:T(8,128)S(1)} %convolution_add_fusion.7), channel_id=1, replica_groups=mesh['tm'=16,'blk'=8,'samp'=2] {'blk'}, dimensions={1}, use_global_device_ids=true | all-gather | bytes 36864 | tf_op jit(solution)/shard_map/all_gather | solution.py:108
  424.2 18.2 %all_gather.73 = f32[2,8,1024]{2,1,0:T(8,128)S(1)} all-gather(f32[2,8,128]{2,1,0:T(8,128)S(1)} %fusion.18), channel_id=1, replica_groups=mesh['tm'=16,'blk'=8,'samp'=2] {'blk'}, dimensions={2}, use_global_device_ids=true | all-gather | bytes 73728 | tf_op jit(solution)/shard_map/all_gather | solution.py:117
  442.9 18.1 %all_gather.74 = f32[8,1024]{1,0:T(8,128)S(1)} all-gather(f32[8,128]{1,0:T(8,128)S(1)} %fusion.19), channel_id=1, replica_groups=mesh['tm'=16,'blk'=8,'samp'=2] {'blk'}, dimensions={1}, use_global_device_ids=true | all-gather | bytes 36864 | tf_op jit(solution)/shard_map/all_gather | solution.py:121
  461.3 483.5 %while.14 = (s32[]{:T(128)}, f32[8,1024]{1,0:T(8,128)S(1)}, f32[128,1024]{1,0:T(8,128)S(1)}, f32[8,128]{1,0:T(8,128)S(1)}, s32[]{:T(128)}, /*index=5*/s32[]{:T(128)}, u32[]{:T(128)}, u32[]{:T(128)}, s32[]{:T(128)}) while((s32[]{:T(128)}, f32[8,1024]{1,0:T(8,128)S(1)}, f32[128,1024]{1,0:T(8,128)S(1)}, f32[8,128]{1,0:T(8,128)S(1)}, ...), condition=%wide.region_2.3_spmd.clone, body=%wide.region_1.2_spmd.clone.sunk | while | flops 12608520 | bytes 831686 | solution.py:130
  461.8 18.2 %all_gather.77 = f32[8,1024]{1,0:T(8,128)S(1)} all-gather(f32[8,128]{1,0:T(8,128)S(1)} %convolution_add_fusion.12), channel_id=1, replica_groups=mesh['tm'=16,'blk'=8,'samp'=2] {'blk'}, dimensions={1}, use_global_device_ids=true | all-gather | bytes 36864 | tf_op jit(solution)/shard_map/while/body/eval_jaxpr/all_gather | solution.py:126
  480.0 57.5 %collective-permute-start = (f32[8,1024]{1,0:T(8,128)S(1)}, f32[8,1024]{1,0:T(8,128)S(1)}, u32[]{:S(2)}, u32[]{:S(2)}) collective-permute-start(f32[8,1024]{1,0:T(8,128)S(1)} %all_gather.77), channel_id=1, source_target_pairs={{16,0},{32,16},{48,32},{64,48},{80,64},{96,80},{112,96},{128,112},... | collective-permute-start | bytes 98312 | tf_op jit(solution)/shard_map/while/body/eval_jaxpr/ppermute | solution.py:25
  546.5 18.2 %all_gather.77 = f32[8,1024]{1,0:T(8,128)S(1)} all-gather(f32[8,128]{1,0:T(8,128)S(1)} %convolution_add_fusion.12), channel_id=1, replica_groups=mesh['tm'=16,'blk'=8,'samp'=2] {'blk'}, dimensions={1}, use_global_device_ids=true | all-gather | bytes 36864 | tf_op jit(solution)/shard_map/while/body/eval_jaxpr/all_gather | solution.py:126
  575.0 18.2 %all_gather.77 = f32[8,1024]{1,0:T(8,128)S(1)} all-gather(f32[8,128]{1,0:T(8,128)S(1)} %convolution_add_fusion.12), channel_id=1, replica_groups=mesh['tm'=16,'blk'=8,'samp'=2] {'blk'}, dimensions={1}, use_global_device_ids=true | all-gather | bytes 36864 | tf_op jit(solution)/shard_map/while/body/eval_jaxpr/all_gather | solution.py:126
  603.4 18.2 %all_gather.77 = f32[8,1024]{1,0:T(8,128)S(1)} all-gather(f32[8,128]{1,0:T(8,128)S(1)} %convolution_add_fusion.12), channel_id=1, replica_groups=mesh['tm'=16,'blk'=8,'samp'=2] {'blk'}, dimensions={1}, use_global_device_ids=true | all-gather | bytes 36864 | tf_op jit(solution)/shard_map/while/body/eval_jaxpr/all_gather | solution.py:126
  631.9 18.2 %all_gather.77 = f32[8,1024]{1,0:T(8,128)S(1)} all-gather(f32[8,128]{1,0:T(8,128)S(1)} %convolution_add_fusion.12), channel_id=1, replica_groups=mesh['tm'=16,'blk'=8,'samp'=2] {'blk'}, dimensions={1}, use_global_device_ids=true | all-gather | bytes 36864 | tf_op jit(solution)/shard_map/while/body/eval_jaxpr/all_gather | solution.py:126
  660.4 18.2 %all_gather.77 = f32[8,1024]{1,0:T(8,128)S(1)} all-gather(f32[8,128]{1,0:T(8,128)S(1)} %convolution_add_fusion.12), channel_id=1, replica_groups=mesh['tm'=16,'blk'=8,'samp'=2] {'blk'}, dimensions={1}, use_global_device_ids=true | all-gather | bytes 36864 | tf_op jit(solution)/shard_map/while/body/eval_jaxpr/all_gather | solution.py:126
  688.9 18.2 %all_gather.77 = f32[8,1024]{1,0:T(8,128)S(1)} all-gather(f32[8,128]{1,0:T(8,128)S(1)} %convolution_add_fusion.12), channel_id=1, replica_groups=mesh['tm'=16,'blk'=8,'samp'=2] {'blk'}, dimensions={1}, use_global_device_ids=true | all-gather | bytes 36864 | tf_op jit(solution)/shard_map/while/body/eval_jaxpr/all_gather | solution.py:126
  717.4 18.2 %all_gather.77 = f32[8,1024]{1,0:T(8,128)S(1)} all-gather(f32[8,128]{1,0:T(8,128)S(1)} %convolution_add_fusion.12), channel_id=1, replica_groups=mesh['tm'=16,'blk'=8,'samp'=2] {'blk'}, dimensions={1}, use_global_device_ids=true | all-gather | bytes 36864 | tf_op jit(solution)/shard_map/while/body/eval_jaxpr/all_gather | solution.py:126
  745.9 18.2 %all_gather.77 = f32[8,1024]{1,0:T(8,128)S(1)} all-gather(f32[8,128]{1,0:T(8,128)S(1)} %convolution_add_fusion.12), channel_id=1, replica_groups=mesh['tm'=16,'blk'=8,'samp'=2] {'blk'}, dimensions={1}, use_global_device_ids=true | all-gather | bytes 36864 | tf_op jit(solution)/shard_map/while/body/eval_jaxpr/all_gather | solution.py:126
  774.3 18.2 %all_gather.77 = f32[8,1024]{1,0:T(8,128)S(1)} all-gather(f32[8,128]{1,0:T(8,128)S(1)} %convolution_add_fusion.12), channel_id=1, replica_groups=mesh['tm'=16,'blk'=8,'samp'=2] {'blk'}, dimensions={1}, use_global_device_ids=true | all-gather | bytes 36864 | tf_op jit(solution)/shard_map/while/body/eval_jaxpr/all_gather | solution.py:126
  802.8 18.2 %all_gather.77 = f32[8,1024]{1,0:T(8,128)S(1)} all-gather(f32[8,128]{1,0:T(8,128)S(1)} %convolution_add_fusion.12), channel_id=1, replica_groups=mesh['tm'=16,'blk'=8,'samp'=2] {'blk'}, dimensions={1}, use_global_device_ids=true | all-gather | bytes 36864 | tf_op jit(solution)/shard_map/while/body/eval_jaxpr/all_gather | solution.py:126
  831.3 18.2 %all_gather.77 = f32[8,1024]{1,0:T(8,128)S(1)} all-gather(f32[8,128]{1,0:T(8,128)S(1)} %convolution_add_fusion.12), channel_id=1, replica_groups=mesh['tm'=16,'blk'=8,'samp'=2] {'blk'}, dimensions={1}, use_global_device_ids=true | all-gather | bytes 36864 | tf_op jit(solution)/shard_map/while/body/eval_jaxpr/all_gather | solution.py:126
  859.8 18.2 %all_gather.77 = f32[8,1024]{1,0:T(8,128)S(1)} all-gather(f32[8,128]{1,0:T(8,128)S(1)} %convolution_add_fusion.12), channel_id=1, replica_groups=mesh['tm'=16,'blk'=8,'samp'=2] {'blk'}, dimensions={1}, use_global_device_ids=true | all-gather | bytes 36864 | tf_op jit(solution)/shard_map/while/body/eval_jaxpr/all_gather | solution.py:126
  888.3 18.2 %all_gather.77 = f32[8,1024]{1,0:T(8,128)S(1)} all-gather(f32[8,128]{1,0:T(8,128)S(1)} %convolution_add_fusion.12), channel_id=1, replica_groups=mesh['tm'=16,'blk'=8,'samp'=2] {'blk'}, dimensions={1}, use_global_device_ids=true | all-gather | bytes 36864 | tf_op jit(solution)/shard_map/while/body/eval_jaxpr/all_gather | solution.py:126
  916.8 18.2 %all_gather.77 = f32[8,1024]{1,0:T(8,128)S(1)} all-gather(f32[8,128]{1,0:T(8,128)S(1)} %convolution_add_fusion.12), channel_id=1, replica_groups=mesh['tm'=16,'blk'=8,'samp'=2] {'blk'}, dimensions={1}, use_global_device_ids=true | all-gather | bytes 36864 | tf_op jit(solution)/shard_map/while/body/eval_jaxpr/all_gather | solution.py:126
  (171 shorter events, 261.0 us)
Async XLA Ops:
  6.5 51.7 %all-gather.17.cloned.1.call-start = ((), (), s32[]{:S(2)}) async-start(), calls=%async_computation.4 | async-start | bytes 2359296 | tf_op jit(solution)/shard_map/all_gather | solution.py:80
  16.1 271.2 %copy-start = (bf16[2,128,1024]{2,1,0:T(8,128)(2,1)}, bf16[2,128,1024]{2,1,0:T(8,128)(2,1)S(1)}, u32[]{:S(2)}) copy-start(bf16[2,128,1024]{2,1,0:T(8,128)(2,1)S(1)} %all_gather.63) | copy-start | bytes 1572868
  16.9 123.9 %all-gather.9.cloned.1.call-start = ((), (), s32[]{:S(2)}) async-start(), calls=%async_computation | async-start | bytes 4718592 | tf_op jit(solution)/shard_map/all_gather | solution.py:101
  60.3 13.5 %collective-permute-start.5 = (f32[128,1024]{1,0:T(8,128)S(1)}, f32[128,1024]{1,0:T(8,128)S(1)}, u32[]{:S(2)}, u32[]{:S(2)}) collective-permute-start(f32[128,1024]{1,0:T(8,128)S(1)} %fusion.4), channel_id=1, source_target_pairs={{0,16},{16,32},{32,48},{48,64},{64,80},{80,96},{96,112},{112,128},... | collective-permute-start | bytes 1572872 | tf_op jit(solution)/shard_map/ppermute | solution.py:25
  73.7 12.6 %collective-permute-start.7 = (f32[128,1024]{1,0:T(8,128)S(1)}, f32[128,1024]{1,0:T(8,128)S(1)}, u32[]{:S(2)}, u32[]{:S(2)}) collective-permute-start(f32[128,1024]{1,0:T(8,128)S(1)} %collective-permute-done.5), channel_id=1, source_target_pairs={{0,16},{16,32},{32,48},{48,64},{64,80},{80,96},{96,112},{112,128},... | collective-permute-start | bytes 1572872 | tf_op jit(solution)/shard_map/ppermute | solution.py:25
  87.2 128.5 %all-gather.11.cloned.1.call-start = ((), (), s32[]{:S(2)}) async-start(), calls=%async_computation.1 | async-start | bytes 4718592 | tf_op jit(solution)/shard_map/all_gather | solution.py:101
  145.5 14.8 %collective-permute-start.9 = (f32[128,1024]{1,0:T(8,128)S(1)}, f32[128,1024]{1,0:T(8,128)S(1)}, u32[]{:S(2)}, u32[]{:S(2)}) collective-permute-start(f32[128,1024]{1,0:T(8,128)S(1)} %fusion.29), channel_id=1, source_target_pairs={{0,32},{16,48},{32,64},{48,80},{64,96},{80,112},{96,128},{112,144}... | collective-permute-start | bytes 1572872 | tf_op jit(solution)/shard_map/ppermute | solution.py:25
  161.2 218.6 %all-gather.15.cloned.1.call-start = ((), (), s32[]{:S(2)}) async-start(), calls=%async_computation.3 | async-start | bytes 2359296 | tf_op jit(solution)/shard_map/all_gather | solution.py:85
  170.5 229.5 %all-gather.13.cloned.1.call-start = ((), (), s32[]{:S(2)}) async-start(), calls=%async_computation.2 | async-start | bytes 4718592 | tf_op jit(solution)/shard_map/all_gather | solution.py:101
  220.2 16.2 %collective-permute-start.11 = (f32[128,1024]{1,0:T(8,128)S(1)}, f32[128,1024]{1,0:T(8,128)S(1)}, u32[]{:S(2)}, u32[]{:S(2)}) collective-permute-start(f32[128,1024]{1,0:T(8,128)S(1)} %fusion.30), channel_id=1, source_target_pairs={{0,64},{16,80},{32,96},{48,112},{64,128},{80,144},{96,160},{112,17... | collective-permute-start | bytes 1572872 | tf_op jit(solution)/shard_map/ppermute | solution.py:25
  237.4 8.5 collective-permute-start.1
  237.4 8.5 collective-permute-start.2
  287.5 17.6 %collective-permute-start.3 = (f32[8,128]{1,0:T(8,128)S(1)}, f32[8,128]{1,0:T(8,128)S(1)}, u32[]{:S(2)}, u32[]{:S(2)}) collective-permute-start(f32[8,128]{1,0:T(8,128)S(1)} %convolution_add_fusion.4), channel_id=1, source_target_pairs={{0,16},{16,32},{32,48},{48,64},{64,80},{80,96},{96,112},{112,128},... | collective-permute-start | bytes 12296 | tf_op jit(solution)/shard_map/ppermute | solution.py:25
  305.1 7.0 collective-permute-start.4
  330.6 4.4 collective-permute-start.6
  353.6 5.9 collective-permute-start.8
  378.3 3.5 collective-permute-start.10
  480.0 66.1 %collective-permute-start = (f32[8,1024]{1,0:T(8,128)S(1)}, f32[8,1024]{1,0:T(8,128)S(1)}, u32[]{:S(2)}, u32[]{:S(2)}) collective-permute-start(f32[8,1024]{1,0:T(8,128)S(1)} %all_gather.77), channel_id=1, source_target_pairs={{16,0},{32,16},{48,32},{64,48},{80,64},{96,80},{112,96},{128,112},... | collective-permute-start | bytes 98312 | tf_op jit(solution)/shard_map/while/body/eval_jaxpr/ppermute | solution.py:25
  564.7 9.9 %collective-permute-start = (f32[8,1024]{1,0:T(8,128)S(1)}, f32[8,1024]{1,0:T(8,128)S(1)}, u32[]{:S(2)}, u32[]{:S(2)}) collective-permute-start(f32[8,1024]{1,0:T(8,128)S(1)} %all_gather.77), channel_id=1, source_target_pairs={{16,0},{32,16},{48,32},{64,48},{80,64},{96,80},{112,96},{128,112},... | collective-permute-start | bytes 98312 | tf_op jit(solution)/shard_map/while/body/eval_jaxpr/ppermute | solution.py:25
  593.1 9.9 %collective-permute-start = (f32[8,1024]{1,0:T(8,128)S(1)}, f32[8,1024]{1,0:T(8,128)S(1)}, u32[]{:S(2)}, u32[]{:S(2)}) collective-permute-start(f32[8,1024]{1,0:T(8,128)S(1)} %all_gather.77), channel_id=1, source_target_pairs={{16,0},{32,16},{48,32},{64,48},{80,64},{96,80},{112,96},{128,112},... | collective-permute-start | bytes 98312 | tf_op jit(solution)/shard_map/while/body/eval_jaxpr/ppermute | solution.py:25
  621.6 9.9 %collective-permute-start = (f32[8,1024]{1,0:T(8,128)S(1)}, f32[8,1024]{1,0:T(8,128)S(1)}, u32[]{:S(2)}, u32[]{:S(2)}) collective-permute-start(f32[8,1024]{1,0:T(8,128)S(1)} %all_gather.77), channel_id=1, source_target_pairs={{16,0},{32,16},{48,32},{64,48},{80,64},{96,80},{112,96},{128,112},... | collective-permute-start | bytes 98312 | tf_op jit(solution)/shard_map/while/body/eval_jaxpr/ppermute | solution.py:25
  650.1 9.9 %collective-permute-start = (f32[8,1024]{1,0:T(8,128)S(1)}, f32[8,1024]{1,0:T(8,128)S(1)}, u32[]{:S(2)}, u32[]{:S(2)}) collective-permute-start(f32[8,1024]{1,0:T(8,128)S(1)} %all_gather.77), channel_id=1, source_target_pairs={{16,0},{32,16},{48,32},{64,48},{80,64},{96,80},{112,96},{128,112},... | collective-permute-start | bytes 98312 | tf_op jit(solution)/shard_map/while/body/eval_jaxpr/ppermute | solution.py:25
  678.6 9.9 %collective-permute-start = (f32[8,1024]{1,0:T(8,128)S(1)}, f32[8,1024]{1,0:T(8,128)S(1)}, u32[]{:S(2)}, u32[]{:S(2)}) collective-permute-start(f32[8,1024]{1,0:T(8,128)S(1)} %all_gather.77), channel_id=1, source_target_pairs={{16,0},{32,16},{48,32},{64,48},{80,64},{96,80},{112,96},{128,112},... | collective-permute-start | bytes 98312 | tf_op jit(solution)/shard_map/while/body/eval_jaxpr/ppermute | solution.py:25
  707.1 9.9 %collective-permute-start = (f32[8,1024]{1,0:T(8,128)S(1)}, f32[8,1024]{1,0:T(8,128)S(1)}, u32[]{:S(2)}, u32[]{:S(2)}) collective-permute-start(f32[8,1024]{1,0:T(8,128)S(1)} %all_gather.77), channel_id=1, source_target_pairs={{16,0},{32,16},{48,32},{64,48},{80,64},{96,80},{112,96},{128,112},... | collective-permute-start | bytes 98312 | tf_op jit(solution)/shard_map/while/body/eval_jaxpr/ppermute | solution.py:25
  735.6 9.9 %collective-permute-start = (f32[8,1024]{1,0:T(8,128)S(1)}, f32[8,1024]{1,0:T(8,128)S(1)}, u32[]{:S(2)}, u32[]{:S(2)}) collective-permute-start(f32[8,1024]{1,0:T(8,128)S(1)} %all_gather.77), channel_id=1, source_target_pairs={{16,0},{32,16},{48,32},{64,48},{80,64},{96,80},{112,96},{128,112},... | collective-permute-start | bytes 98312 | tf_op jit(solution)/shard_map/while/body/eval_jaxpr/ppermute | solution.py:25
  764.0 9.9 %collective-permute-start = (f32[8,1024]{1,0:T(8,128)S(1)}, f32[8,1024]{1,0:T(8,128)S(1)}, u32[]{:S(2)}, u32[]{:S(2)}) collective-permute-start(f32[8,1024]{1,0:T(8,128)S(1)} %all_gather.77), channel_id=1, source_target_pairs={{16,0},{32,16},{48,32},{64,48},{80,64},{96,80},{112,96},{128,112},... | collective-permute-start | bytes 98312 | tf_op jit(solution)/shard_map/while/body/eval_jaxpr/ppermute | solution.py:25
  792.5 9.9 %collective-permute-start = (f32[8,1024]{1,0:T(8,128)S(1)}, f32[8,1024]{1,0:T(8,128)S(1)}, u32[]{:S(2)}, u32[]{:S(2)}) collective-permute-start(f32[8,1024]{1,0:T(8,128)S(1)} %all_gather.77), channel_id=1, source_target_pairs={{16,0},{32,16},{48,32},{64,48},{80,64},{96,80},{112,96},{128,112},... | collective-permute-start | bytes 98312 | tf_op jit(solution)/shard_map/while/body/eval_jaxpr/ppermute | solution.py:25
  821.0 9.9 %collective-permute-start = (f32[8,1024]{1,0:T(8,128)S(1)}, f32[8,1024]{1,0:T(8,128)S(1)}, u32[]{:S(2)}, u32[]{:S(2)}) collective-permute-start(f32[8,1024]{1,0:T(8,128)S(1)} %all_gather.77), channel_id=1, source_target_pairs={{16,0},{32,16},{48,32},{64,48},{80,64},{96,80},{112,96},{128,112},... | collective-permute-start | bytes 98312 | tf_op jit(solution)/shard_map/while/body/eval_jaxpr/ppermute | solution.py:25
  849.5 9.9 %collective-permute-start = (f32[8,1024]{1,0:T(8,128)S(1)}, f32[8,1024]{1,0:T(8,128)S(1)}, u32[]{:S(2)}, u32[]{:S(2)}) collective-permute-start(f32[8,1024]{1,0:T(8,128)S(1)} %all_gather.77), channel_id=1, source_target_pairs={{16,0},{32,16},{48,32},{64,48},{80,64},{96,80},{112,96},{128,112},... | collective-permute-start | bytes 98312 | tf_op jit(solution)/shard_map/while/body/eval_jaxpr/ppermute | solution.py:25
  878.0 9.9 %collective-permute-start = (f32[8,1024]{1,0:T(8,128)S(1)}, f32[8,1024]{1,0:T(8,128)S(1)}, u32[]{:S(2)}, u32[]{:S(2)}) collective-permute-start(f32[8,1024]{1,0:T(8,128)S(1)} %all_gather.77), channel_id=1, source_target_pairs={{16,0},{32,16},{48,32},{64,48},{80,64},{96,80},{112,96},{128,112},... | collective-permute-start | bytes 98312 | tf_op jit(solution)/shard_map/while/body/eval_jaxpr/ppermute | solution.py:25
  906.5 9.9 %collective-permute-start = (f32[8,1024]{1,0:T(8,128)S(1)}, f32[8,1024]{1,0:T(8,128)S(1)}, u32[]{:S(2)}, u32[]{:S(2)}) collective-permute-start(f32[8,1024]{1,0:T(8,128)S(1)} %all_gather.77), channel_id=1, source_target_pairs={{16,0},{32,16},{48,32},{64,48},{80,64},{96,80},{112,96},{128,112},... | collective-permute-start | bytes 98312 | tf_op jit(solution)/shard_map/while/body/eval_jaxpr/ppermute | solution.py:25
  934.9 9.9 %collective-permute-start = (f32[8,1024]{1,0:T(8,128)S(1)}, f32[8,1024]{1,0:T(8,128)S(1)}, u32[]{:S(2)}, u32[]{:S(2)}) collective-permute-start(f32[8,1024]{1,0:T(8,128)S(1)} %all_gather.77), channel_id=1, source_target_pairs={{16,0},{32,16},{48,32},{64,48},{80,64},{96,80},{112,96},{128,112},... | collective-permute-start | bytes 98312 | tf_op jit(solution)/shard_map/while/body/eval_jaxpr/ppermute | solution.py:25
  (16 other events, 1222.5 us)
Sparse Core Ops, SparseCore 0:
  17.0 41.1 all-gather.16
  87.3 53.4 all-gather.8
  161.3 54.2 all-gather.10
  217.3 36.5 all-gather.14
  255.5 56.7 all-gather.12
where the time goes:
time: 954 us; the launch traced here: 953 us
  blocking collectives  463 us (49%)
  waiting for transfers between devices  301 us (32%)
  starting transfers between devices  137 us (14%)
  matrix products  29.7 us (3%)
  between operations  13.6 us (1%)
    all_gather x15, blocking collectives, relay_back(): complete = lax.all_gather(emitted, 'blk', axis=1, tiled=True)  273 us
    ppermute x24, waiting for transfers between devices, shifted(): lax.ppermute(value, axis, [(source, source + steps) for source in range(i...  161 us
    ppermute x24, starting transfers between devices, shifted(): lax.ppermute(value, axis, [(source, source + steps) for source in range(i...  134 us
    all_gather x3, waiting for transfers between devices, on_device(): lax.all_gather(received_m, 'blk', axis=0, tiled=True)  98.7 us
    all_gather x4, blocking collectives, on_device(): lax.all_gather(received_v, 'blk', axis=1, tiled=True)  72.5 us
    all_gather x1, waiting for transfers between devices, on_device(): lax.all_gather(trans_mats[0], 'blk', axis=0, tiled=True)  41.3 us
    all_gather x1, blocking collectives, on_device(): lax.all_gather(inputs[0], 'blk', axis=1, tiled=True)  20.3 us
    all_gather x1, blocking collectives, on_device(): all_resid = lax.all_gather(residual, 'blk', axis=2, tiled=True)  19.8 us
  transfers between devices with their start and end apart: 31, of which 26 were waited for; matrix products, arithmetic and copies ran while one was open for 1% of the time, Pallas kernels for 0%

commit v1 on v0

--- a/solution.py
+++ b/solution.py
@@ -86,7 +86,9 @@
         preferred_element_type=jnp.float32,
     )
     first_input, initial = (
-        lax.all_gather(inputs[0], "blk", axis=1, tiled=True),
+        jnp.concatenate(
+            lax.all_to_all(jnp.stack([inputs[0]] * lax.axis_size("blk")), "blk", 0, 0), axis=1
+        ),
         lax.all_gather(start_mean, "blk", axis=1, tiled=True),
     )
     carry_input = apply_rows(trans_mats[1], first_input) + inputs[1]

time: 954 us -> 942 us (0.987)
    all_gather x1 -> x0, blocking collectives: 20.3 us -> none  [on_device(): lax.all_gather(inputs[0], 'blk', axis=1, tiled=True)]
    all_to_all x0 -> x1, blocking collectives: none -> 10.7 us  [on_device(): lax.all_to_all(jnp.stack([inputs[0]] * lax.axis_size('blk')), 'blk', 0, 0)]
where the time goes in v1:
time: 942 us; the launch traced here: 941 us
  blocking collectives  455 us (48%)
  waiting for transfers between devices  301 us (32%)
  starting transfers between devices  134 us (14%)
  matrix products  29.7 us (3%)
  between operations  13.6 us (1%)
    all_gather x15, blocking collectives, relay_back(): complete = lax.all_gather(emitted, 'blk', axis=1, tiled=True)  273 us
    ppermute x24, waiting for transfers between devices, shifted(): lax.ppermute(value, axis, [(source, source + steps) for source in range(i...  160 us
    ppermute x24, starting transfers between devices, shifted(): lax.ppermute(value, axis, [(source, source + steps) for source in range(i...  131 us
    all_gather x3, waiting for transfers between devices, on_device(): lax.all_gather(received_m, 'blk', axis=0, tiled=True)  98.7 us
    all_gather x4, blocking collectives, on_device(): lax.all_gather(received_v, 'blk', axis=1, tiled=True)  73.6 us
    all_gather x1, waiting for transfers between devices, on_device(): lax.all_gather(trans_mats[0], 'blk', axis=0, tiled=True)  41.3 us
    all_gather x1, blocking collectives, on_device(): all_resid = lax.all_gather(residual, 'blk', axis=2, tiled=True)  19.8 us
  transfers between devices with their start and end apart: 31, of which 26 were waited for; matrix products, arithmetic and copies ran while one was open for 1% of the time, Pallas kernels for 0%

profile of v1, /device:TPU:7, one launch (start us, length us, event | category | flops | bytes accessed | tf_op | source)
XLA Modules:
  0.0 940.7 jit_solution(2164384760626639911)
XLA Ops:
  16.9 41.3 %all-gather.16.cloned.1.call-done = bf16[1,1024,1024]{2,1,0:T(8,128)(2,1)} async-done(((bf16[1,128,1024]{2,1,0:T(8,128)(2,1)}), bf16[1,1024,1024]{2,1,0:T(8,128)(2,1)}) %all-gather.16.cloned.1.call-update) | async-done | bytes 2097168 | tf_op jit(solution)/shard_map/all_gather | solution.py:80
  87.2 53.6 %all-gather.8.cloned.1.call-done = f32[1024,1024]{1,0:T(8,128)} async-done(((f32[128,1024]{1,0:T(8,128)}), f32[1024,1024]{1,0:T(8,128)}) %all-gather.8.cloned.1.call-update) | async-done | bytes 4194320 | tf_op jit(solution)/shard_map/all_gather | solution.py:103
  148.7 11.6 %collective-permute-done.9 = f32[128,1024]{1,0:T(8,128)S(1)} collective-permute-done((f32[128,1024]{1,0:T(8,128)S(1)}, f32[128,1024]{1,0:T(8,128)S(1)}, u32[]{:S(2)}, u32[]{:S(2)}) %collective-permute-start.9) | collective-permute-done | bytes 524320 | tf_op jit(solution)/shard_map/ppermute | solution.py:25
  170.5 45.1 %all-gather.10.cloned.1.call-done = f32[1024,1024]{1,0:T(8,128)} async-done(((f32[128,1024]{1,0:T(8,128)}), f32[1024,1024]{1,0:T(8,128)}) %all-gather.10.cloned.1.call-update) | async-done | bytes 4194320 | tf_op jit(solution)/shard_map/all_gather | solution.py:103
  224.2 12.2 %collective-permute-done.11 = f32[128,1024]{1,0:T(8,128)S(1)} collective-permute-done((f32[128,1024]{1,0:T(8,128)S(1)}, f32[128,1024]{1,0:T(8,128)S(1)}, u32[]{:S(2)}, u32[]{:S(2)}) %collective-permute-start.11) | collective-permute-done | bytes 524320 | tf_op jit(solution)/shard_map/ppermute | solution.py:25
  246.9 19.8 %all_gather.57 = f32[2,8,256]{1,0,2:T(2,128)S(1)} all-gather(f32[2,8,32]{1,0,2:T(2,128)S(1)} %copy.27), channel_id=1, replica_groups=mesh['tm'=16,'blk'=8,'samp'=2] {'blk'}, dimensions={2}, use_global_device_ids=true | all-gather | bytes 18432 | tf_op jit(solution)/shard_map/all_gather | solution.py:74
  267.0 10.7 %all_to_all.5 = f32[8,8,128]{2,1,0:T(8,128)S(1)} all-to-all(f32[8,8,128]{2,1,0:T(8,128)S(1)} %stack.21), channel_id=1, replica_groups=mesh['tm'=16,'blk'=8,'samp'=2] {'blk'}, dimensions={0} | all-to-all | bytes 65536 | tf_op jit(solution)/shard_map/all_to_all | solution.py:90
  278.0 14.3 %collective-permute-start.3 = (f32[8,128]{1,0:T(8,128)S(1)}, f32[8,128]{1,0:T(8,128)S(1)}, u32[]{:S(2)}, u32[]{:S(2)}) collective-permute-start(f32[8,128]{1,0:T(8,128)S(1)} %convolution_add_fusion.4), channel_id=1, source_target_pairs={{0,16},{16,32},{32,48},{48,64},{64,80},{80,96},{96,112},{112,128},... | collective-permute-start | bytes 12296 | tf_op jit(solution)/shard_map/ppermute | solution.py:25
  300.0 19.3 %all_gather.60 = f32[8,1024]{1,0:T(8,128)S(1)} all-gather(f32[8,128]{1,0:T(8,128)S(1)} %collective-permute-done.4), channel_id=1, replica_groups=mesh['tm'=16,'blk'=8,'samp'=2] {'blk'}, dimensions={1}, use_global_device_ids=true | all-gather | bytes 36864 | tf_op jit(solution)/shard_map/all_gather | solution.py:104
  324.2 18.1 %all_gather.62 = f32[8,1024]{1,0:T(8,128)S(1)} all-gather(f32[8,128]{1,0:T(8,128)S(1)} %collective-permute-done.6), channel_id=1, replica_groups=mesh['tm'=16,'blk'=8,'samp'=2] {'blk'}, dimensions={1}, use_global_device_ids=true | all-gather | bytes 36864 | tf_op jit(solution)/shard_map/all_gather | solution.py:104
  348.7 18.1 %all_gather.64 = f32[8,1024]{1,0:T(8,128)S(1)} all-gather(f32[8,128]{1,0:T(8,128)S(1)} %collective-permute-done.8), channel_id=1, replica_groups=mesh['tm'=16,'blk'=8,'samp'=2] {'blk'}, dimensions={1}, use_global_device_ids=true | all-gather | bytes 36864 | tf_op jit(solution)/shard_map/all_gather | solution.py:104
  370.8 18.1 %all_gather.66 = f32[8,1024]{1,0:T(8,128)S(1)} all-gather(f32[8,128]{1,0:T(8,128)S(1)} %collective-permute-done.10), channel_id=1, replica_groups=mesh['tm'=16,'blk'=8,'samp'=2] {'blk'}, dimensions={1}, use_global_device_ids=true | all-gather | bytes 36864 | tf_op jit(solution)/shard_map/all_gather | solution.py:104
  393.9 18.2 %all_gather.68 = f32[8,1024]{1,0:T(8,128)S(1)} all-gather(f32[8,128]{1,0:T(8,128)S(1)} %convolution_add_fusion.7), channel_id=1, replica_groups=mesh['tm'=16,'blk'=8,'samp'=2] {'blk'}, dimensions={1}, use_global_device_ids=true | all-gather | bytes 36864 | tf_op jit(solution)/shard_map/all_gather | solution.py:110
  413.2 18.2 %all_gather.69 = f32[2,8,1024]{2,1,0:T(8,128)S(1)} all-gather(f32[2,8,128]{2,1,0:T(8,128)S(1)} %fusion.18), channel_id=1, replica_groups=mesh['tm'=16,'blk'=8,'samp'=2] {'blk'}, dimensions={2}, use_global_device_ids=true | all-gather | bytes 73728 | tf_op jit(solution)/shard_map/all_gather | solution.py:119
  431.9 18.1 %all_gather.70 = f32[8,1024]{1,0:T(8,128)S(1)} all-gather(f32[8,128]{1,0:T(8,128)S(1)} %fusion.19), channel_id=1, replica_groups=mesh['tm'=16,'blk'=8,'samp'=2] {'blk'}, dimensions={1}, use_global_device_ids=true | all-gather | bytes 36864 | tf_op jit(solution)/shard_map/all_gather | solution.py:123
  450.2 482.5 %while.14 = (s32[]{:T(128)}, f32[8,1024]{1,0:T(8,128)S(1)}, f32[128,1024]{1,0:T(8,128)S(1)}, f32[8,128]{1,0:T(8,128)S(1)}, s32[]{:T(128)}, /*index=5*/s32[]{:T(128)}, u32[]{:T(128)}, u32[]{:T(128)}, s32[]{:T(128)}) while((s32[]{:T(128)}, f32[8,1024]{1,0:T(8,128)S(1)}, f32[128,1024]{1,0:T(8,128)S(1)}, f32[8,128]{1,0:T(8,128)S(1)}, ...), condition=%wide.region_2.3_spmd.clone, body=%wide.region_1.2_spmd.clone.sunk | while | flops 12608520 | bytes 831686 | solution.py:132
  450.8 18.2 %all_gather.73 = f32[8,1024]{1,0:T(8,128)S(1)} all-gather(f32[8,128]{1,0:T(8,128)S(1)} %convolution_add_fusion.12), channel_id=1, replica_groups=mesh['tm'=16,'blk'=8,'samp'=2] {'blk'}, dimensions={1}, use_global_device_ids=true | all-gather | bytes 36864 | tf_op jit(solution)/shard_map/while/body/eval_jaxpr/all_gather | solution.py:128
  468.9 56.4 %collective-permute-start = (f32[8,1024]{1,0:T(8,128)S(1)}, f32[8,1024]{1,0:T(8,128)S(1)}, u32[]{:S(2)}, u32[]{:S(2)}) collective-permute-start(f32[8,1024]{1,0:T(8,128)S(1)} %all_gather.73), channel_id=1, source_target_pairs={{16,0},{32,16},{48,32},{64,48},{80,64},{96,80},{112,96},{128,112},... | collective-permute-start | bytes 98312 | tf_op jit(solution)/shard_map/while/body/eval_jaxpr/ppermute | solution.py:25
  534.4 18.2 %all_gather.73 = f32[8,1024]{1,0:T(8,128)S(1)} all-gather(f32[8,128]{1,0:T(8,128)S(1)} %convolution_add_fusion.12), channel_id=1, replica_groups=mesh['tm'=16,'blk'=8,'samp'=2] {'blk'}, dimensions={1}, use_global_device_ids=true | all-gather | bytes 36864 | tf_op jit(solution)/shard_map/while/body/eval_jaxpr/all_gather | solution.py:128
  562.9 18.2 %all_gather.73 = f32[8,1024]{1,0:T(8,128)S(1)} all-gather(f32[8,128]{1,0:T(8,128)S(1)} %convolution_add_fusion.12), channel_id=1, replica_groups=mesh['tm'=16,'blk'=8,'samp'=2] {'blk'}, dimensions={1}, use_global_device_ids=true | all-gather | bytes 36864 | tf_op jit(solution)/shard_map/while/body/eval_jaxpr/all_gather | solution.py:128
  591.4 18.2 %all_gather.73 = f32[8,1024]{1,0:T(8,128)S(1)} all-gather(f32[8,128]{1,0:T(8,128)S(1)} %convolution_add_fusion.12), channel_id=1, replica_groups=mesh['tm'=16,'blk'=8,'samp'=2] {'blk'}, dimensions={1}, use_global_device_ids=true | all-gather | bytes 36864 | tf_op jit(solution)/shard_map/while/body/eval_jaxpr/all_gather | solution.py:128
  619.9 18.2 %all_gather.73 = f32[8,1024]{1,0:T(8,128)S(1)} all-gather(f32[8,128]{1,0:T(8,128)S(1)} %convolution_add_fusion.12), channel_id=1, replica_groups=mesh['tm'=16,'blk'=8,'samp'=2] {'blk'}, dimensions={1}, use_global_device_ids=true | all-gather | bytes 36864 | tf_op jit(solution)/shard_map/while/body/eval_jaxpr/all_gather | solution.py:128
  648.3 18.2 %all_gather.73 = f32[8,1024]{1,0:T(8,128)S(1)} all-gather(f32[8,128]{1,0:T(8,128)S(1)} %convolution_add_fusion.12), channel_id=1, replica_groups=mesh['tm'=16,'blk'=8,'samp'=2] {'blk'}, dimensions={1}, use_global_device_ids=true | all-gather | bytes 36864 | tf_op jit(solution)/shard_map/while/body/eval_jaxpr/all_gather | solution.py:128
  676.8 18.2 %all_gather.73 = f32[8,1024]{1,0:T(8,128)S(1)} all-gather(f32[8,128]{1,0:T(8,128)S(1)} %convolution_add_fusion.12), channel_id=1, replica_groups=mesh['tm'=16,'blk'=8,'samp'=2] {'blk'}, dimensions={1}, use_global_device_ids=true | all-gather | bytes 36864 | tf_op jit(solution)/shard_map/while/body/eval_jaxpr/all_gather | solution.py:128
  705.3 18.2 %all_gather.73 = f32[8,1024]{1,0:T(8,128)S(1)} all-gather(f32[8,128]{1,0:T(8,128)S(1)} %convolution_add_fusion.12), channel_id=1, replica_groups=mesh['tm'=16,'blk'=8,'samp'=2] {'blk'}, dimensions={1}, use_global_device_ids=true | all-gather | bytes 36864 | tf_op jit(solution)/shard_map/while/body/eval_jaxpr/all_gather | solution.py:128
  733.8 18.2 %all_gather.73 = f32[8,1024]{1,0:T(8,128)S(1)} all-gather(f32[8,128]{1,0:T(8,128)S(1)} %convolution_add_fusion.12), channel_id=1, replica_groups=mesh['tm'=16,'blk'=8,'samp'=2] {'blk'}, dimensions={1}, use_global_device_ids=true | all-gather | bytes 36864 | tf_op jit(solution)/shard_map/while/body/eval_jaxpr/all_gather | solution.py:128
  762.3 18.2 %all_gather.73 = f32[8,1024]{1,0:T(8,128)S(1)} all-gather(f32[8,128]{1,0:T(8,128)S(1)} %convolution_add_fusion.12), channel_id=1, replica_groups=mesh['tm'=16,'blk'=8,'samp'=2] {'blk'}, dimensions={1}, use_global_device_ids=true | all-gather | bytes 36864 | tf_op jit(solution)/shard_map/while/body/eval_jaxpr/all_gather | solution.py:128
  790.8 18.2 %all_gather.73 = f32[8,1024]{1,0:T(8,128)S(1)} all-gather(f32[8,128]{1,0:T(8,128)S(1)} %convolution_add_fusion.12), channel_id=1, replica_groups=mesh['tm'=16,'blk'=8,'samp'=2] {'blk'}, dimensions={1}, use_global_device_ids=true | all-gather | bytes 36864 | tf_op jit(solution)/shard_map/while/body/eval_jaxpr/all_gather | solution.py:128
  819.2 18.2 %all_gather.73 = f32[8,1024]{1,0:T(8,128)S(1)} all-gather(f32[8,128]{1,0:T(8,128)S(1)} %convolution_add_fusion.12), channel_id=1, replica_groups=mesh['tm'=16,'blk'=8,'samp'=2] {'blk'}, dimensions={1}, use_global_device_ids=true | all-gather | bytes 36864 | tf_op jit(solution)/shard_map/while/body/eval_jaxpr/all_gather | solution.py:128
  847.7 18.2 %all_gather.73 = f32[8,1024]{1,0:T(8,128)S(1)} all-gather(f32[8,128]{1,0:T(8,128)S(1)} %convolution_add_fusion.12), channel_id=1, replica_groups=mesh['tm'=16,'blk'=8,'samp'=2] {'blk'}, dimensions={1}, use_global_device_ids=true | all-gather | bytes 36864 | tf_op jit(solution)/shard_map/while/body/eval_jaxpr/all_gather | solution.py:128
  876.2 18.2 %all_gather.73 = f32[8,1024]{1,0:T(8,128)S(1)} all-gather(f32[8,128]{1,0:T(8,128)S(1)} %convolution_add_fusion.12), channel_id=1, replica_groups=mesh['tm'=16,'blk'=8,'samp'=2] {'blk'}, dimensions={1}, use_global_device_ids=true | all-gather | bytes 36864 | tf_op jit(solution)/shard_map/while/body/eval_jaxpr/all_gather | solution.py:128
  904.7 18.2 %all_gather.73 = f32[8,1024]{1,0:T(8,128)S(1)} all-gather(f32[8,128]{1,0:T(8,128)S(1)} %convolution_add_fusion.12), channel_id=1, replica_groups=mesh['tm'=16,'blk'=8,'samp'=2] {'blk'}, dimensions={1}, use_global_device_ids=true | all-gather | bytes 36864 | tf_op jit(solution)/shard_map/while/body/eval_jaxpr/all_gather | solution.py:128
  (172 shorter events, 261.1 us)
Async XLA Ops:
  6.5 51.7 %all-gather.16.cloned.1.call-start = ((), (), s32[]{:S(2)}) async-start(), calls=%async_computation.5 | async-start | bytes 2359296 | tf_op jit(solution)/shard_map/all_gather | solution.py:80
  16.1 261.7 %copy-start = (bf16[2,128,1024]{2,1,0:T(8,128)(2,1)}, bf16[2,128,1024]{2,1,0:T(8,128)(2,1)S(1)}, u32[]{:S(2)}) copy-start(bf16[2,128,1024]{2,1,0:T(8,128)(2,1)S(1)} %all_gather.59) | copy-start | bytes 1572868
  16.9 123.9 %all-gather.8.cloned.1.call-start = ((), (), s32[]{:S(2)}) async-start(), calls=%async_computation.1 | async-start | bytes 4718592 | tf_op jit(solution)/shard_map/all_gather | solution.py:103
  60.3 13.5 %collective-permute-start.5 = (f32[128,1024]{1,0:T(8,128)S(1)}, f32[128,1024]{1,0:T(8,128)S(1)}, u32[]{:S(2)}, u32[]{:S(2)}) collective-permute-start(f32[128,1024]{1,0:T(8,128)S(1)} %fusion.4), channel_id=1, source_target_pairs={{0,16},{16,32},{32,48},{48,64},{64,80},{80,96},{96,112},{112,128},... | collective-permute-start | bytes 1572872 | tf_op jit(solution)/shard_map/ppermute | solution.py:25
  73.7 12.6 %collective-permute-start.7 = (f32[128,1024]{1,0:T(8,128)S(1)}, f32[128,1024]{1,0:T(8,128)S(1)}, u32[]{:S(2)}, u32[]{:S(2)}) collective-permute-start(f32[128,1024]{1,0:T(8,128)S(1)} %collective-permute-done.5), channel_id=1, source_target_pairs={{0,16},{16,32},{32,48},{48,64},{64,80},{80,96},{96,112},{112,128},... | collective-permute-start | bytes 1572872 | tf_op jit(solution)/shard_map/ppermute | solution.py:25
  87.2 128.5 %all-gather.10.cloned.1.call-start = ((), (), s32[]{:S(2)}) async-start(), calls=%async_computation.2 | async-start | bytes 4718592 | tf_op jit(solution)/shard_map/all_gather | solution.py:103
  145.5 14.8 %collective-permute-start.9 = (f32[128,1024]{1,0:T(8,128)S(1)}, f32[128,1024]{1,0:T(8,128)S(1)}, u32[]{:S(2)}, u32[]{:S(2)}) collective-permute-start(f32[128,1024]{1,0:T(8,128)S(1)} %fusion.29), channel_id=1, source_target_pairs={{0,32},{16,48},{32,64},{48,80},{64,96},{80,112},{96,128},{112,144}... | collective-permute-start | bytes 1572872 | tf_op jit(solution)/shard_map/ppermute | solution.py:25
  161.2 207.6 %all-gather.14.cloned.1.call-start = ((), (), s32[]{:S(2)}) async-start(), calls=%async_computation.4 | async-start | bytes 2359296 | tf_op jit(solution)/shard_map/all_gather | solution.py:85
  170.5 218.5 %all-gather.12.cloned.1.call-start = ((), (), s32[]{:S(2)}) async-start(), calls=%async_computation.3 | async-start | bytes 4718592 | tf_op jit(solution)/shard_map/all_gather | solution.py:103
  220.2 16.2 %collective-permute-start.11 = (f32[128,1024]{1,0:T(8,128)S(1)}, f32[128,1024]{1,0:T(8,128)S(1)}, u32[]{:S(2)}, u32[]{:S(2)}) collective-permute-start(f32[128,1024]{1,0:T(8,128)S(1)} %fusion.30), channel_id=1, source_target_pairs={{0,64},{16,80},{32,96},{48,112},{64,128},{80,144},{96,160},{112,17... | collective-permute-start | bytes 1572872 | tf_op jit(solution)/shard_map/ppermute | solution.py:25
  237.4 8.5 collective-permute-start.1
  237.4 8.5 collective-permute-start.2
  278.0 15.0 %collective-permute-start.3 = (f32[8,128]{1,0:T(8,128)S(1)}, f32[8,128]{1,0:T(8,128)S(1)}, u32[]{:S(2)}, u32[]{:S(2)}) collective-permute-start(f32[8,128]{1,0:T(8,128)S(1)} %convolution_add_fusion.4), channel_id=1, source_target_pairs={{0,16},{16,32},{32,48},{48,64},{64,80},{80,96},{96,112},{112,128},... | collective-permute-start | bytes 12296 | tf_op jit(solution)/shard_map/ppermute | solution.py:25
  293.0 7.0 collective-permute-start.4
  319.8 4.4 collective-permute-start.6
  342.7 5.9 collective-permute-start.8
  367.3 3.5 collective-permute-start.10
  468.9 65.0 %collective-permute-start = (f32[8,1024]{1,0:T(8,128)S(1)}, f32[8,1024]{1,0:T(8,128)S(1)}, u32[]{:S(2)}, u32[]{:S(2)}) collective-permute-start(f32[8,1024]{1,0:T(8,128)S(1)} %all_gather.73), channel_id=1, source_target_pairs={{16,0},{32,16},{48,32},{64,48},{80,64},{96,80},{112,96},{128,112},... | collective-permute-start | bytes 98312 | tf_op jit(solution)/shard_map/while/body/eval_jaxpr/ppermute | solution.py:25
  552.6 9.9 %collective-permute-start = (f32[8,1024]{1,0:T(8,128)S(1)}, f32[8,1024]{1,0:T(8,128)S(1)}, u32[]{:S(2)}, u32[]{:S(2)}) collective-permute-start(f32[8,1024]{1,0:T(8,128)S(1)} %all_gather.73), channel_id=1, source_target_pairs={{16,0},{32,16},{48,32},{64,48},{80,64},{96,80},{112,96},{128,112},... | collective-permute-start | bytes 98312 | tf_op jit(solution)/shard_map/while/body/eval_jaxpr/ppermute | solution.py:25
  581.1 9.9 %collective-permute-start = (f32[8,1024]{1,0:T(8,128)S(1)}, f32[8,1024]{1,0:T(8,128)S(1)}, u32[]{:S(2)}, u32[]{:S(2)}) collective-permute-start(f32[8,1024]{1,0:T(8,128)S(1)} %all_gather.73), channel_id=1, source_target_pairs={{16,0},{32,16},{48,32},{64,48},{80,64},{96,80},{112,96},{128,112},... | collective-permute-start | bytes 98312 | tf_op jit(solution)/shard_map/while/body/eval_jaxpr/ppermute | solution.py:25
  609.6 9.9 %collective-permute-start = (f32[8,1024]{1,0:T(8,128)S(1)}, f32[8,1024]{1,0:T(8,128)S(1)}, u32[]{:S(2)}, u32[]{:S(2)}) collective-permute-start(f32[8,1024]{1,0:T(8,128)S(1)} %all_gather.73), channel_id=1, source_target_pairs={{16,0},{32,16},{48,32},{64,48},{80,64},{96,80},{112,96},{128,112},... | collective-permute-start | bytes 98312 | tf_op jit(solution)/shard_map/while/body/eval_jaxpr/ppermute | solution.py:25
  638.0 9.9 %collective-permute-start = (f32[8,1024]{1,0:T(8,128)S(1)}, f32[8,1024]{1,0:T(8,128)S(1)}, u32[]{:S(2)}, u32[]{:S(2)}) collective-permute-start(f32[8,1024]{1,0:T(8,128)S(1)} %all_gather.73), channel_id=1, source_target_pairs={{16,0},{32,16},{48,32},{64,48},{80,64},{96,80},{112,96},{128,112},... | collective-permute-start | bytes 98312 | tf_op jit(solution)/shard_map/while/body/eval_jaxpr/ppermute | solution.py:25
  666.5 9.9 %collective-permute-start = (f32[8,1024]{1,0:T(8,128)S(1)}, f32[8,1024]{1,0:T(8,128)S(1)}, u32[]{:S(2)}, u32[]{:S(2)}) collective-permute-start(f32[8,1024]{1,0:T(8,128)S(1)} %all_gather.73), channel_id=1, source_target_pairs={{16,0},{32,16},{48,32},{64,48},{80,64},{96,80},{112,96},{128,112},... | collective-permute-start | bytes 98312 | tf_op jit(solution)/shard_map/while/body/eval_jaxpr/ppermute | solution.py:25
  695.0 9.9 %collective-permute-start = (f32[8,1024]{1,0:T(8,128)S(1)}, f32[8,1024]{1,0:T(8,128)S(1)}, u32[]{:S(2)}, u32[]{:S(2)}) collective-permute-start(f32[8,1024]{1,0:T(8,128)S(1)} %all_gather.73), channel_id=1, source_target_pairs={{16,0},{32,16},{48,32},{64,48},{80,64},{96,80},{112,96},{128,112},... | collective-permute-start | bytes 98312 | tf_op jit(solution)/shard_map/while/body/eval_jaxpr/ppermute | solution.py:25
  723.5 9.9 %collective-permute-start = (f32[8,1024]{1,0:T(8,128)S(1)}, f32[8,1024]{1,0:T(8,128)S(1)}, u32[]{:S(2)}, u32[]{:S(2)}) collective-permute-start(f32[8,1024]{1,0:T(8,128)S(1)} %all_gather.73), channel_id=1, source_target_pairs={{16,0},{32,16},{48,32},{64,48},{80,64},{96,80},{112,96},{128,112},... | collective-permute-start | bytes 98312 | tf_op jit(solution)/shard_map/while/body/eval_jaxpr/ppermute | solution.py:25
  752.0 9.9 %collective-permute-start = (f32[8,1024]{1,0:T(8,128)S(1)}, f32[8,1024]{1,0:T(8,128)S(1)}, u32[]{:S(2)}, u32[]{:S(2)}) collective-permute-start(f32[8,1024]{1,0:T(8,128)S(1)} %all_gather.73), channel_id=1, source_target_pairs={{16,0},{32,16},{48,32},{64,48},{80,64},{96,80},{112,96},{128,112},... | collective-permute-start | bytes 98312 | tf_op jit(solution)/shard_map/while/body/eval_jaxpr/ppermute | solution.py:25
  780.5 9.9 %collective-permute-start = (f32[8,1024]{1,0:T(8,128)S(1)}, f32[8,1024]{1,0:T(8,128)S(1)}, u32[]{:S(2)}, u32[]{:S(2)}) collective-permute-start(f32[8,1024]{1,0:T(8,128)S(1)} %all_gather.73), channel_id=1, source_target_pairs={{16,0},{32,16},{48,32},{64,48},{80,64},{96,80},{112,96},{128,112},... | collective-permute-start | bytes 98312 | tf_op jit(solution)/shard_map/while/body/eval_jaxpr/ppermute | solution.py:25
  808.9 9.9 %collective-permute-start = (f32[8,1024]{1,0:T(8,128)S(1)}, f32[8,1024]{1,0:T(8,128)S(1)}, u32[]{:S(2)}, u32[]{:S(2)}) collective-permute-start(f32[8,1024]{1,0:T(8,128)S(1)} %all_gather.73), channel_id=1, source_target_pairs={{16,0},{32,16},{48,32},{64,48},{80,64},{96,80},{112,96},{128,112},... | collective-permute-start | bytes 98312 | tf_op jit(solution)/shard_map/while/body/eval_jaxpr/ppermute | solution.py:25
  837.4 9.9 %collective-permute-start = (f32[8,1024]{1,0:T(8,128)S(1)}, f32[8,1024]{1,0:T(8,128)S(1)}, u32[]{:S(2)}, u32[]{:S(2)}) collective-permute-start(f32[8,1024]{1,0:T(8,128)S(1)} %all_gather.73), channel_id=1, source_target_pairs={{16,0},{32,16},{48,32},{64,48},{80,64},{96,80},{112,96},{128,112},... | collective-permute-start | bytes 98312 | tf_op jit(solution)/shard_map/while/body/eval_jaxpr/ppermute | solution.py:25
  865.9 9.9 %collective-permute-start = (f32[8,1024]{1,0:T(8,128)S(1)}, f32[8,1024]{1,0:T(8,128)S(1)}, u32[]{:S(2)}, u32[]{:S(2)}) collective-permute-start(f32[8,1024]{1,0:T(8,128)S(1)} %all_gather.73), channel_id=1, source_target_pairs={{16,0},{32,16},{48,32},{64,48},{80,64},{96,80},{112,96},{128,112},... | collective-permute-start | bytes 98312 | tf_op jit(solution)/shard_map/while/body/eval_jaxpr/ppermute | solution.py:25
  894.4 9.9 %collective-permute-start = (f32[8,1024]{1,0:T(8,128)S(1)}, f32[8,1024]{1,0:T(8,128)S(1)}, u32[]{:S(2)}, u32[]{:S(2)}) collective-permute-start(f32[8,1024]{1,0:T(8,128)S(1)} %all_gather.73), channel_id=1, source_target_pairs={{16,0},{32,16},{48,32},{64,48},{80,64},{96,80},{112,96},{128,112},... | collective-permute-start | bytes 98312 | tf_op jit(solution)/shard_map/while/body/eval_jaxpr/ppermute | solution.py:25
  922.9 9.9 %collective-permute-start = (f32[8,1024]{1,0:T(8,128)S(1)}, f32[8,1024]{1,0:T(8,128)S(1)}, u32[]{:S(2)}, u32[]{:S(2)}) collective-permute-start(f32[8,1024]{1,0:T(8,128)S(1)} %all_gather.73), channel_id=1, source_target_pairs={{16,0},{32,16},{48,32},{64,48},{80,64},{96,80},{112,96},{128,112},... | collective-permute-start | bytes 98312 | tf_op jit(solution)/shard_map/while/body/eval_jaxpr/ppermute | solution.py:25
  (16 other events, 1200.0 us)
Sparse Core Ops, SparseCore 0:
  17.0 41.1 all-gather.15
  87.3 53.4 all-gather.7
  161.3 54.2 all-gather.9
  217.3 36.5 all-gather.13
  255.5 57.3 all-gather.11
